TPU v7x, 512 devices: a whole 4x4x16 slice. The times are simulated.
512 devices in a mesh: pair: 16 (over x, z_lo), side: 2 (over core), rows: 16 (over z_hi, y).
Axes of the slice: x: 4, y: 4, z: 16 (z_hi: 4, z_lo: 4; z = z_hi * 4 + z_lo), core: 2. Of those that a mesh axis runs over, the one named last changes fastest.
Arguments:
- face_out: float32 [16, 2048, 768], P('pair', ('side', 'rows')), as said below
- face_in: float32 [16, 768, 7680], P('pair', 'rows', 'side'), as said below
- face_shared: float32 [16, 2, 768, 768], P('pair', 'side', 'rows'), as said below
Outputs:
- correction_t: float32 [16, 2, 3840, 2048], P('pair', None, 'rows', 'side')
- mean_square: float32 [], replicated
Inputs may be any that keep to these rules, and one draw needn't show every extreme that they name: `face_out`: float entries of order one over the square root of 768 or less. `face_in`: float entries. `face_shared`: each block is symmetric and positive definite, so the sum of a pair's two blocks is too.
All inputs are finite; a program needn't handle non-finite values.
Results may differ from a plain program's by a relative error of at most 0.0003.
Values sent between devices are 32-bit elements; how exact they have to be, the bound alone decides.
A program may use at most 64 MiB of HBM per device.

v0:
```python
import jax
import jax.numpy as jnp
from jax import lax
from jax.sharding import PartitionSpec as P


def transposed_product(solved_cols, piece):
    return -lax.dot_general(
        solved_cols,
        piece,
        (((0,), (1,)), ((), ())),
        precision=lax.Precision.HIGHEST,
        preferred_element_type=jnp.float32,
    )


def body(face_out, face_in, face_shared):
    panel = face_out[0]
    shared = face_shared[0, 0]
    summed = lax.psum(shared, "side")
    schur = lax.all_gather(summed, "rows", axis=0, tiled=True)
    factor = jnp.linalg.cholesky(schur)
    columns = lax.all_to_all(face_in[0], "rows", split_axis=1, concat_axis=0, tiled=True)
    solved = jax.scipy.linalg.cho_solve((factor, True), columns)
    width = solved.shape[1]
    own_columns = transposed_product(
        solved, lax.all_gather(panel, ("side", "rows"), axis=0, tiled=True)
    )
    merged = lax.all_to_all(own_columns, "side", split_axis=1, concat_axis=0, tiled=True)
    block = jnp.reshape(merged, (2, width, merged.shape[1]))
    total = lax.psum(jnp.sum(block * block), ("pair", "side", "rows"))
    entries = block.size * lax.axis_size("pair") * lax.axis_size("side") * lax.axis_size("rows")
    return (block[None], total / entries)


def solution(mesh):
    in_specs = (
        P("pair", ("side", "rows"), None),
        P("pair", "rows", "side"),
        P("pair", "side", "rows", None),
    )
    out_specs = (P("pair", None, "rows", "side"), P())
    return jax.shard_map(body, mesh=mesh, in_specs=in_specs, out_specs=out_specs, check_vma=False)
```

profile of v0, /device:TPU:1, one launch (start us, length us, event | category | flops | bytes accessed | tf_op | source)
XLA Modules:
  0.0 554.0 jit_solution(6917689189741116257)
XLA Ops:
  7.2 0.7 all-reduce.3.cloned.1.call-update
  7.9 48.7 %all-reduce.3.cloned.1.call-done = f32[48,768]{1,0:T(8,128)} async-done(((f32[48,768]{1,0:T(8,128)}), f32[48,768]{1,0:T(8,128)}) %all-reduce.3.cloned.1.call-update) | async-done | bytes 147472 | tf_op jit(solution)/shard_map/psum | solution.py:20
  56.7 1.9 all_to_all.26
  58.6 1.3 copy.13
  60.0 13.5 %all-to-all-start = ((f32[48,16,240]{2,0,1:T(8,128)}), f32[48,16,240]{2,0,1:T(8,128)S(1)}, u32[]{:S(2)}, u32[]{:S(2)}) async-start(f32[48,16,240]{2,0,1:T(8,128)} %copy.13), calls=%async_computation | async-start | bytes 1572864 | tf_op jit(solution)/shard_map/all_to_all | solution.py:23
  73.5 0.7 all-gather.6.cloned.1.call-update
  74.2 48.8 %all-to-all-done = f32[48,16,240]{2,0,1:T(8,128)S(1)} async-done(((f32[48,16,240]{2,0,1:T(8,128)}), f32[48,16,240]{2,0,1:T(8,128)S(1)}, u32[]{:S(2)}, u32[]{:S(2)}) %all-to-all-start) | async-done | bytes 737312 | tf_op jit(solution)/shard_map/all_to_all | solution.py:23
  123.1 0.8 copy.20
  123.9 0.7 copy.21
  124.6 0.7 copy.22
  125.3 0.7 copy.23
  126.1 0.7 copy.24
  126.8 58.8 %all-gather.4.cloned.1.call-done = f32[768,768]{1,0:T(8,128)} async-done(((f32[48,768]{1,0:T(8,128)}), f32[768,768]{1,0:T(8,128)}) %all-gather.4.cloned.1.call-update) | async-done | bytes 2359312 | tf_op jit(solution)/shard_map/all_gather | solution.py:21
  185.7 3.4 copy.12
  189.1 2.0 fusion.5
  191.1 1.4 copy-done.2
  192.5 11.7 %cholesky.165 = f32[128,128]{1,0:T(8,128)S(1)} custom-call(f32[128,128]{1,0:T(8,128)S(1)} %cholesky.424), custom_call_target="Cholesky" | custom-call | tf_op jit(solution)/shard_map/jit(cholesky)/cholesky | solution.py:22
  204.2 9.8 %custom-call.50 = f32[1,128,128]{1,2,0:T(8,128)S(1)} custom-call(f32[1,128,128]{2,1,0:T(8,128)S(1)} %get-tuple-element.40), custom_call_target="InvertDiagBlocksLowerTriangular" | custom-call | tf_op jit(solution)/shard_map/jit(cholesky)/cholesky | solution.py:22
  214.2 1.4 constant_dynamic-update-slice_fusion.20
  215.6 1.4 convolution_subtract_fusion
  217.0 0.6 cholesky.428
  217.6 12.5 %cholesky.188 = f32[128,128]{1,0:T(8,128)S(1)} custom-call(f32[128,128]{1,0:T(8,128)} %cholesky.428), custom_call_target="Cholesky" | custom-call | tf_op jit(solution)/shard_map/jit(cholesky)/cholesky | solution.py:22
  230.2 0.6 select_reduce_fusion.4
  230.8 10.8 %custom-call.51 = f32[1,128,128]{1,2,0:T(8,128)S(1)} custom-call(f32[1,128,128]{2,1,0:T(8,128)} %get-tuple-element.37), custom_call_target="InvertDiagBlocksLowerTriangular" | custom-call | tf_op jit(solution)/shard_map/jit(cholesky)/cholesky | solution.py:22
  242.0 1.5 convolution_subtract_fusion.1
  243.6 11.7 %cholesky.354 = f32[128,128]{1,0:T(8,128)S(1)} custom-call(f32[128,128]{1,0:T(8,128)S(1)} %cholesky.433), custom_call_target="Cholesky" | custom-call | tf_op jit(solution)/shard_map/jit(cholesky)/cholesky | solution.py:22
  255.3 9.8 %custom-call.52 = f32[1,128,128]{1,2,0:T(8,128)S(1)} custom-call(f32[1,128,128]{2,1,0:T(8,128)S(1)} %get-tuple-element.34), custom_call_target="InvertDiagBlocksLowerTriangular" | custom-call | tf_op jit(solution)/shard_map/jit(cholesky)/cholesky | solution.py:22
  265.4 1.6 convolution_subtract_fusion.2
  267.0 12.1 %cholesky.373 = f32[128,128]{1,0:T(8,128)S(1)} custom-call(f32[128,128]{1,0:T(8,128)S(1)} %cholesky.438), custom_call_target="Cholesky" | custom-call | tf_op jit(solution)/shard_map/jit(cholesky)/cholesky | solution.py:22
  279.1 9.8 %custom-call.53 = f32[1,128,128]{1,2,0:T(8,128)S(1)} custom-call(f32[1,128,128]{2,1,0:T(8,128)S(1)} %get-tuple-element.31), custom_call_target="InvertDiagBlocksLowerTriangular" | custom-call | tf_op jit(solution)/shard_map/jit(cholesky)/cholesky | solution.py:22
  289.2 1.5 convolution_subtract_fusion.3
  290.7 11.7 %cholesky.392 = f32[128,128]{1,0:T(8,128)S(1)} custom-call(f32[128,128]{1,0:T(8,128)S(1)} %cholesky.443), custom_call_target="Cholesky" | custom-call | tf_op jit(solution)/shard_map/jit(cholesky)/cholesky | solution.py:22
  302.5 9.8 %custom-call.54 = f32[1,128,128]{1,2,0:T(8,128)S(1)} custom-call(f32[1,128,128]{2,1,0:T(8,128)S(1)} %get-tuple-element.28), custom_call_target="InvertDiagBlocksLowerTriangular" | custom-call | tf_op jit(solution)/shard_map/jit(cholesky)/cholesky | solution.py:22
  312.5 1.3 convolution_subtract_fusion.14
  313.8 11.9 %cholesky.410 = f32[128,128]{1,0:T(8,128)S(1)} custom-call(f32[128,128]{1,0:T(8,128)S(1)} %convolution_subtract_fusion.14), custom_call_target="Cholesky" | custom-call | tf_op jit(solution)/shard_map/jit(cholesky)/cholesky | solution.py:22
  325.7 0.7 compare_reduce_fusion.4
  327.6 0.6 compare_reduce_fusion.3
  328.8 0.6 compare_reduce_fusion.2
  330.0 0.6 compare_reduce_fusion.1
  331.3 0.6 compare_reduce_fusion
  332.5 1.6 select_select_fusion
  334.1 20.4 %while.1 = (s32[]{:T(128)}, f32[768,768]{1,0:T(8,128)}, s32[6,2]{0,1:T(2,128)S(1)}, f32[6,128,128]{2,1,0:T(8,128)}, s32[]{:T(128)}) while((s32[]{:T(128)}, f32[768,768]{1,0:T(8,128)}, s32[6,2]{0,1:T(2,128)S(1)}, f32[6,128,128]{2,1,0:T(8,128)}, s32[]{:T(128)}) %tuple.45), condition=%wide.while_cond, body=%wide.while_body.sunk | while | flops 2 | bytes 132705 | solution.py:24
  334.2 0.5 fusion.104
  334.7 2.8 bitcast_dynamic-update-slice_fusion.2
  337.6 0.5 fusion.104
  338.1 2.8 bitcast_dynamic-update-slice_fusion.2
  341.5 2.8 bitcast_dynamic-update-slice_fusion.2
  345.0 2.8 bitcast_dynamic-update-slice_fusion.2
  347.8 0.5 fusion.104
  348.4 2.8 bitcast_dynamic-update-slice_fusion.2
  351.8 2.7 bitcast_dynamic-update-slice_fusion.2
  354.5 59.9 %custom-call.55 = f32[6,128,128]{1,2,0:T(8,128)S(1)} custom-call(f32[6,128,128]{2,1,0:T(8,128)} %get-tuple-element.9), custom_call_target="InvertDiagBlocksLowerTriangular" | custom-call | tf_op jit(solution)/shard_map/jit(_cho_solve)/triangular_solve | solution.py:24
  414.8 1.2 convolution_subtract_fusion.9
  416.4 1.3 convolution_subtract_fusion.11
  418.0 1.4 convolution_subtract_fusion.13
  419.6 0.6 convolution_subtract_fusion.8
  420.5 0.7 convolution_subtract_fusion.7
  423.6 0.6 convolution_subtract_fusion.5
  424.6 0.7 convolution_subtract_fusion.4
  425.6 7.7 %fusion.2 = f32[240,2048]{1,0:T(8,128)S(1)} fusion(f32[768,240]{0,1:T(8,128)S(1)} %constant_dynamic-update-slice_fusion.10, f32[1,2048,768]{2,1,0:T(8,128)} %all-gather.6.cloned.1.call-done), kind=kOutput, calls=%fused_computation.4 | convolution fusion | flops 4530339840 | bytes 8994816 | tf_op jit(solution)/shard_map/dot_general | solution.py:8
  433.5 9.0 %all_to_all.35 = f32[240,2,1024]{2,0,1:T(8,128)S(1)} all-to-all(f32[240,2,1024]{2,0,1:T(8,128)S(1)} %bitcast.115), channel_id=1, replica_groups=mesh['pair'=16,'side'=2,'rows'=16] {'side'}, dimensions={1} | all-to-all | bytes 3932160 | tf_op jit(solution)/shard_map/all_to_all | solution.py:29
  442.6 1.1 fusion.6
  443.7 100.5 %psum.15 = f32[]{:T(128)} all-reduce(f32[]{:T(128)} %fusion.6), channel_id=1, replica_groups=mesh['pair'=16,'side'=2,'rows'=16] {'pair','side','rows'}, use_global_device_ids=true, to_apply=%region_14.15 | all-reduce | flops 1 | bytes 8 | tf_op jit(solution)/shard_map/psum | solution.py:31
  544.8 1.3 copy.63
  (66 shorter events, 8.4 us)
Async XLA Ops:
  7.2 49.5 %all-reduce.3.cloned.1.call-start = ((), (), s32[]{:S(2)}) async-start(), calls=%async_computation.2 | async-start | bytes 294912 | tf_op jit(solution)/shard_map/psum | solution.py:20
  7.9 177.8 %all-gather.4.cloned.1.call-start = ((), (), s32[]{:S(2)}) async-start(), calls=%async_computation.3 | async-start | bytes 2506752 | tf_op jit(solution)/shard_map/all_gather | solution.py:21
  60.0 63.1 %all-to-all-start = ((f32[48,16,240]{2,0,1:T(8,128)}), f32[48,16,240]{2,0,1:T(8,128)S(1)}, u32[]{:S(2)}, u32[]{:S(2)}) async-start(f32[48,16,240]{2,0,1:T(8,128)} %copy.13), calls=%async_computation | async-start | bytes 1572864 | tf_op jit(solution)/shard_map/all_to_all | solution.py:23
  73.4 352.2 %all-gather.6.cloned.1.call-start = ((), (), s32[]{:S(2)}) async-start(), calls=%async_computation.4 | async-start | bytes 6488064 | tf_op jit(solution)/shard_map/all_gather | solution.py:27
  185.7 3.4 copy-start
  191.0 1.4 copy-start.2
  354.5 63.5 %copy-start.1 = (f32[768,768]{1,0:T(8,128)S(1)}, f32[768,768]{1,0:T(8,128)}, u32[]{:S(2)}) copy-start(f32[768,768]{1,0:T(8,128)} %get-tuple-element.109) | copy-start | bytes 7077892
  414.4 5.2 copy-start.4
  414.8 5.6 %copy-start.3 = (f32[128,240]{0,1:T(8,128)S(1)}, f32[128,240]{0,1:T(8,128)}, u32[]{:S(2)}) copy-start(f32[128,240]{0,1:T(8,128)} %copy.24) | copy-start | bytes 368644
Sparse Core Ops, SparseCore 0:
  10.8 45.7 all-reduce.2
  59.7 125.9 all-gather.3
  188.8 115.8 all-gather.5
where the time goes:
time: 557 us; the launch traced here: 554 us
  other arithmetic  190 us (34%)
  waiting for transfers between devices  158 us (28%)
  blocking collectives  110 us (20%)
  local copies, waits for them, and re-layouts  34.6 us (6%)
  matrix products  28.3 us (5%)
  between operations  19.8 us (4%)
  starting transfers between devices  13.6 us (2%)
    another operation x22, other arithmetic, body(): factor = jnp.linalg.cholesky(schur)  126 us
    psum x1, blocking collectives, body(): total = lax.psum(jnp.sum(block * block), ('pair', 'side', 'rows'))  100 us
    another operation x3, other arithmetic, body(): solved = jax.scipy.linalg.cho_solve((factor, True), columns)  61.5 us
    all_gather x1, waiting for transfers between devices, body(): schur = lax.all_gather(summed, 'rows', axis=0, tiled=True)  58.8 us
    all_to_all x1, waiting for transfers between devices, body(): lax.all_to_all(face_in[0], 'rows', split_axis=1, concat_axis=0, tiled=True)  48.8 us
    psum x1, waiting for transfers between devices, body(): summed = lax.psum(shared, 'side')  48.7 us
    another operation x18, local copies, waits for them, and re-layouts  20.4 us
    all_to_all x1, starting transfers between devices, body(): lax.all_to_all(face_in[0], 'rows', split_axis=1, concat_axis=0, tiled=True)  13.5 us
  transfers between devices with their start and end apart: 4, of which 3 were waited for; matrix products, arithmetic and copies ran while one was open for 43% of the time, Pallas kernels for 0%

commit v1 on v0

v1 whole, which is shorter than its diff:
```python
import jax
import jax.numpy as jnp
from jax import lax
from jax.experimental import pallas as pl
from jax.experimental.pallas import tpu as pltpu
from jax.sharding import PartitionSpec as P

MESH = pl.DeviceIdType.MESH
F32 = jnp.float32
BF16 = jnp.bfloat16
NB = 128
G = 8
Y = 4
ZH = 4
ROWS = Y * ZH
STEPS = ((0, 1), (0, 3), (0, 2), (1, 0), (3, 0), (1, 1), (1, 3), (3, 1), (3, 3), (1, 2), (3, 2), (2, 0), (2, 1), (2, 3), (2, 2))


def sweep_tile(tile):
    row = lax.broadcasted_iota(jnp.int32, (G, NB), 0)
    lane = lax.broadcasted_iota(jnp.int32, (G, NB), 1)
    wide = lax.broadcasted_iota(jnp.int32, (NB, NB), 1)
    for k in range(0, NB, G):
        cols = [jnp.broadcast_to(tile[:, k + u : k + u + 1], (NB, NB)) for u in range(G)]
        d = {(t, u): jnp.broadcast_to(cols[u][k + t : k + t + 1, :], (G, NB)) for u in range(G) for t in range(u + 1)}
        inside = (lane >= k) & (lane < k + G)
        pivots = jnp.where(inside, jnp.where(lane - k == row, -1.0, 0.0), tile[k : k + G, :])
        v = [jnp.broadcast_to(pivots[t : t + 1, :], (G, NB)) for t in range(G)]
        r, low = [None] * G, {}
        for t in range(G):
            r[t] = 1.0 / d[t, t]
            for u in range(t + 1, G):
                low[t, u] = d[t, u] * r[t]
            for u in range(t + 1, G):
                for x in range(u, G):
                    d[u, x] = d[u, x] - low[t, u] * d[t, x]
                v[u] = v[u] - low[t, u] * v[t]
        w = [v[t] * r[t] for t in range(G)]
        for t in range(G - 1, 0, -1):
            for u in range(t):
                w[u] = w[u] - low[u, t] * w[t]
        acc = jnp.where((wide >= k) & (wide < k + G), 0.0, tile)
        for t in range(G):
            acc = acc - cols[t] * jnp.broadcast_to(w[t][0:1, :], (NB, NB))
        packed = w[0]
        for t in range(1, G):
            packed = jnp.where(row == t, w[t], packed)
        tile = jnp.concatenate([x for x in (acc[:k], packed, acc[k + G :]) if x.shape[0]], axis=0)
    return tile


def split(x):
    hi = x.astype(BF16)
    return hi, (x - hi.astype(F32)).astype(BF16)


def dot3(a, b, dims):
    (ah, al), (bh, bl) = a, b
    one = lambda x, y: lax.dot_general(x, y, (dims, ((), ())), preferred_element_type=F32)
    return one(ah, bh) + (one(ah, bl) + one(al, bh))


def kernel(scale, panel_ref, in_ref, shared_ref, out_ref, mean_ref, schur, inv, rows_a, pieces, cols_b, xt_hi, xt_lo,
           half_in, acc, sum_r, sum_p, sum_s, half_s, half_r, sz_s, sz_r, sy_s, sy_r, sx_s, sx_r, az_s, az_r, ay_s, ay_r,
           b_s, b_r, bx_s, bx_r, pr_s, pr_r, pp_s, pp_r, ps_s, ps_r):
    me = lax.axis_index("rows")
    side = lax.axis_index("side")
    pair = lax.axis_index("pair")
    zh, y = me // Y, lax.rem(me, Y)
    n = 768
    half = 24
    width = 240
    pairs = 16

    def at(dz, dy):
        return lax.rem(zh + dz, ZH) * Y + lax.rem(y + dy, Y)

    def back(dz, dy):
        return lax.rem(zh + ZH - dz, ZH) * Y + lax.rem(y + Y - dy, Y)

    sibling = {"side": 1 - side}

    def remote(src, dst, send, recv, device):
        return pltpu.make_async_remote_copy(
            src_ref=src, dst_ref=dst, send_sem=send, recv_sem=recv, device_id=device, device_id_type=MESH
        )

    sends = []

    def send(src, dst, s, r, device):
        copy = remote(src, dst, s, r, device)
        copy.start()
        sends.append(copy)

    def arrived(dst, s, r):
        remote(dst, dst, s, r, sibling).wait_recv()

    barrier = pltpu.get_barrier_semaphore()
    pl.semaphore_signal(barrier, inc=1, device_id=sibling, device_id_type=MESH)
    for dz, dy in STEPS:
        pl.semaphore_signal(barrier, inc=1, device_id={"rows": at(dz, dy)}, device_id_type=MESH)
    for o in range(1, pairs):
        pl.semaphore_signal(barrier, inc=1, device_id={"pair": lax.rem(pair + o, pairs)}, device_id_type=MESH)
    pl.semaphore_wait(barrier, ROWS + pairs - 1)

    def strip(ref, r, s):
        return ref.at[pl.ds(pl.multiple_of((r * 2 + s) * half, 8), half), :]

    def panel_at(r):
        return rows_a.at[pl.ds(pl.multiple_of(r * 64, 64), 64), :]

    def columns_at(s, r):
        return cols_b.at[s, pl.ds(pl.multiple_of(r * 48, 16), 48), :]

    theirs = shared_ref.at[0, 0, pl.ds(pl.multiple_of((1 - side) * half, 8), half), :]
    send(theirs, half_in, half_s, half_r, sibling)
    arrived(half_in, half_s, half_r)
    mine = strip(schur, me, side)
    mine[...] = shared_ref[0, 0, pl.ds(pl.multiple_of(side * half, 8), half), :] + half_in[...]
    for i, dz in enumerate((1, 3, 2)):
        send(mine, mine, sz_s.at[i], sz_r.at[i], {"rows": at(dz, 0)})
    for i, dy in enumerate((1, 3, 2)):
        send(mine, mine, sy_s.at[0, i], sy_r.at[0, i], {"rows": at(0, dy)})
    send(mine, mine, sx_s.at[0], sx_r.at[0], sibling)

    panel = panel_ref.at[0]
    for i, dz in enumerate((1, 3, 2)):
        send(panel, panel_at(me), az_s.at[i], az_r.at[i], {"rows": at(dz, 0)})
    for r in range(ROWS):
        pieces[r, :, 0:width] = in_ref[0, :, r * width : (r + 1) * width]
        pieces[r, :, width:256] = jnp.zeros((48, 256 - width), F32)
    panel_at(me)[...] = panel_ref[0]
    columns_at(side, me)[...] = pieces[me]

    for i, dz in enumerate((1, 3, 2)):
        got = strip(schur, back(dz, 0), side)
        arrived(got, sz_s.at[i], sz_r.at[i])
        for j, dy in enumerate((1, 3, 2)):
            send(got, got, sy_s.at[i + 1, j], sy_r.at[i + 1, j], {"rows": at(0, dy)})
        send(got, got, sx_s.at[i + 1], sx_r.at[i + 1], sibling)
    for j, dy in enumerate((1, 3, 2)):
        send(panel, panel_at(me), ay_s.at[0, j], ay_r.at[0, j], {"rows": at(0, dy)})
    for i, (dz, dy) in enumerate(STEPS):
        send(pieces.at[at(dz, dy)], columns_at(side, me), b_s.at[i], b_r.at[i], {"rows": at(dz, dy)})
    for i, dz in enumerate((0, 1, 3, 2)):
        for j, dy in enumerate((1, 3, 2)):
            got = strip(schur, back(dz, dy), side)
            arrived(got, sy_s.at[i, j], sy_r.at[i, j])
            send(got, got, sx_s.at[4 + i * 3 + j], sx_r.at[4 + i * 3 + j], sibling)
    for i, dz in enumerate((0, 1, 3, 2)):
        arrived(strip(schur, back(dz, 0), 1 - side), sx_s.at[i], sx_r.at[i])
    for i, dz in enumerate((0, 1, 3, 2)):
        for j, dy in enumerate((1, 3, 2)):
            arrived(strip(schur, back(dz, dy), 1 - side), sx_s.at[4 + i * 3 + j], sx_r.at[4 + i * 3 + j])

    def onward_rows(i, dz):
        got = panel_at(back(dz, 0))
        return [
            remote(got, got, ay_s.at[i + 1, j], ay_r.at[i + 1, j], {"rows": at(0, dy)}) for j, dy in enumerate((1, 3, 2))
        ]

    def relay_rows(i, dz):
        arrived(panel_at(back(dz, 0)), az_s.at[i], az_r.at[i])
        for copy in onward_rows(i, dz):
            copy.start()

    def onward_columns(i, dz, dy):
        got = columns_at(side, back(dz, dy))
        return remote(got, got, bx_s.at[i], bx_r.at[i], sibling)

    def own_columns():
        got = columns_at(side, me)
        return remote(got, got, bx_s.at[15], bx_r.at[15], sibling)

    def relay_columns(i, dz, dy):
        arrived(columns_at(side, back(dz, dy)), b_s.at[i], b_r.at[i])
        onward_columns(i, dz, dy).start()

    inv[...] = schur[...]

    @pl.loop(0, n // NB)
    def _(b):
        @pl.when(b == 1)
        def _():
            relay_rows(0, 1)
            relay_rows(1, 3)

        @pl.when(b == 2)
        def _():
            relay_rows(2, 2)

        @pl.when(b == 3)
        def _():
            own_columns().start()
            for i in range(3):
                relay_columns(i, *STEPS[i])

        @pl.when(b == 5)
        def _():
            for i in range(3, 11):
                relay_columns(i, *STEPS[i])

        block = pl.ds(pl.multiple_of(b * NB, NB), NB)
        swept = sweep_tile(inv[block, block])
        eye = lax.broadcasted_iota(jnp.int32, (NB, NB), 0) == lax.broadcasted_iota(jnp.int32, (NB, NB), 1)
        column = inv[:, block]
        inv[block, block] = jnp.where(eye, -1.0, 0.0)
        w = jnp.dot(swept, inv[block, :], precision=lax.Precision.HIGHEST, preferred_element_type=F32)
        inv[:, block] = jnp.zeros((n, NB), F32)
        inv[...] = inv[...] + jnp.dot(column, w, precision=lax.Precision.HIGHEST, preferred_element_type=F32)
        inv[block, :] = -w

    for i in range(11, 15):
        relay_columns(i, *STEPS[i])
    arrived(columns_at(1 - side, me), bx_s.at[15], bx_r.at[15])
    for i, (dz, dy) in enumerate(STEPS):
        arrived(columns_at(1 - side, back(dz, dy)), bx_s.at[i], bx_r.at[i])
    for i, dz in enumerate((0, 1, 3, 2)):
        for j, dy in enumerate((1, 3, 2)):
            arrived(panel_at(back(dz, dy)), ay_s.at[i, j], ay_r.at[i, j])

    inverse = split(inv[...])
    for b in range(2):
        x = dot3(split(cols_b[b].T), inverse, ((1,), (0,)))
        xt_hi[b], xt_lo[b] = split(x)

    acc[...] = jnp.zeros((8, 128), F32)

    @pl.loop(0, 4)
    def _(i):
        tile = pl.ds(pl.multiple_of(i * 256, 256), 256)
        a = split(rows_a[tile, :])
        for b in range(2):
            c = dot3((xt_hi[b], xt_lo[b]), a, ((1,), (1,)))[:width]
            out_ref[0, b, :, tile] = c
            s = jnp.sum((c * c).reshape(width // 8, 8, 256), axis=0)
            acc[...] = acc[...] + (s[:, :128] + s[:, 128:])

    sum_r[me] = acc[...]
    for i, (dz, dy) in enumerate(STEPS):
        send(acc, sum_r.at[me], pr_s.at[i], pr_r.at[i], {"rows": at(dz, dy)})
    for i, (dz, dy) in enumerate(STEPS):
        arrived(sum_r.at[back(dz, dy)], pr_s.at[i], pr_r.at[i])
    sum_p[pair] = jnp.sum(sum_r[...], axis=0)
    for o in range(1, pairs):
        send(sum_p.at[pair], sum_p.at[pair], pp_s.at[o], pp_r.at[o], {"pair": lax.rem(pair + o, pairs)})
    for o in range(1, pairs):
        arrived(sum_p.at[lax.rem(pair + pairs - o, pairs)], pp_s.at[o], pp_r.at[o])
    total = jnp.sum(sum_p[...], axis=0)
    sum_s[side] = total
    send(sum_s.at[side], sum_s.at[side], ps_s, ps_r, sibling)
    arrived(sum_s.at[1 - side], ps_s, ps_r)
    mean_ref[0, 0] = jnp.sum(sum_s[0] + sum_s[1]) * scale
    for i, dz in enumerate((1, 3, 2)):
        sends.extend(onward_rows(i, dz))
    for i, (dz, dy) in enumerate(STEPS):
        sends.append(onward_columns(i, dz, dy))
    sends.append(own_columns())
    for copy in sends:
        copy.wait_send()


def body(face_out, face_in, face_shared):
    dma = pltpu.SemaphoreType.DMA
    vmem = pltpu.VMEM
    sems = [dma, dma, dma((3,)), dma((3,)), dma((4, 3)), dma((4, 3)), dma((16,)), dma((16,)), dma((3,)), dma((3,)), dma((4, 3)),
            dma((4, 3)), dma((15,)), dma((15,)), dma((16,)), dma((16,)), dma((15,)), dma((15,)), dma((16,)), dma((16,)), dma, dma]
    entries = 16 * 2 * 3840 * 2048
    out, mean = pl.pallas_call(
        lambda *refs: kernel(1.0 / entries, *refs),
        out_shape=(jax.ShapeDtypeStruct((1, 2, 240, 1024), F32), jax.ShapeDtypeStruct((1, 1), F32)),
        in_specs=[pl.BlockSpec(memory_space=vmem)] * 3,
        out_specs=(pl.BlockSpec(memory_space=vmem), pl.BlockSpec(memory_space=pltpu.SMEM)),
        scratch_shapes=[vmem((768, 768), F32), vmem((768, 768), F32), vmem((1024, 768), F32), vmem((16, 48, 256), F32),
                        vmem((2, 768, 256), F32), vmem((2, 256, 768), BF16), vmem((2, 256, 768), BF16), vmem((24, 768), F32),
                        vmem((8, 128), F32), vmem((16, 8, 128), F32), vmem((16, 8, 128), F32), vmem((2, 8, 128), F32)] + sems,
        compiler_params=pltpu.CompilerParams(collective_id=0, has_side_effects=True, vmem_limit_bytes=56 << 20),
        name="merge",
    )(face_out, face_in, face_shared)
    return out, mean[0, 0]


def solution(mesh):
    in_specs = (P("pair", ("side", "rows"), None), P("pair", "rows", "side"), P("pair", "side", "rows", None))
    out_specs = (P("pair", None, "rows", "side"), P())
    return jax.shard_map(body, mesh=mesh, in_specs=in_specs, out_specs=out_specs, check_vma=False)
```

time: 557 us -> 157 us (0.28)
  other arithmetic: 190 us -> 0 us
  waiting for transfers between devices: 158 us -> 0 us
  Pallas kernels: 0 us -> 151 us
  blocking collectives: 110 us -> 0 us
  local copies, waits for them, and re-layouts: 34.6 us -> 3.04 us
  matrix products: 28.3 us -> 0 us
  between operations: 19.8 us -> 2.39 us
  starting transfers between devices: 13.6 us -> 0 us
    another operation x25 -> x0, other arithmetic: 187 us -> none  [the longest x22 126 us: body(): factor = jnp.linalg.cholesky(schur)]
    pallas_call x0 -> x1, Pallas kernels: none -> 151 us  [body(): pl.pallas_call(lambda *refs: kernel(1.0 / entries, *refs), out_shape=(jax...]
    psum x1 -> x0, blocking collectives: 100 us -> none  [body(): total = lax.psum(jnp.sum(block * block), ('pair', 'side', 'rows'))]
    all_gather x2 -> x0, waiting for transfers between devices: 58.9 us -> none  [the longest x1 58.8 us: body(): schur = lax.all_gather(summed, 'rows', axis=0, tiled=True)]
    all_to_all x1 -> x0, waiting for transfers between devices: 48.8 us -> none  [body(): lax.all_to_all(face_in[0], 'rows', split_axis=1, concat_axis=0, tiled=True)]
    psum x1 -> x0, waiting for transfers between devices: 48.7 us -> none  [body(): summed = lax.psum(shared, 'side')]
    another operation x28 -> x0, local copies, waits for them, and re-layouts: 21.3 us -> none
    another operation x32 -> x0, matrix products: 20.6 us -> none  [the longest x22 10.8 us: body(): solved = jax.scipy.linalg.cho_solve((factor, True), columns)]
  transfers between devices with their start and end apart: 4 -> 0, of which waited for: 3 -> 0; matrix products, arithmetic and copies ran while one was open for 43% -> 0% of each run, Pallas kernels for 0% -> 0%
where the time goes in v1:
time: 157 us
  Pallas kernels  151 us (96%)
  local copies, waits for them, and re-layouts  3.04 us (2%)
  between operations  2.39 us (2%)
    pallas_call x1, Pallas kernels, body(): pl.pallas_call(lambda *refs: kernel(1.0 / entries, *refs), out_shape=(jax...  151 us

profile of v1, /device:TPU:1, one launch (start us, length us, event | category | flops | bytes accessed | tf_op | source)
XLA Modules:
  0.0 156.7 jit_solution(3073251420624034731)
XLA Ops:
  0.6 151.3 %merge.1 = (f32[1,2,240,1024]{3,2,1,0:T(8,128)}, f32[1,1]{1,0:T(1,128)}) custom-call(f32[1,64,768]{2,1,0:T(8,128)} %refs_0_.1, f32[1,48,3840]{2,1,0:T(8,128)} %refs_1_.1, f32[1,1,48,768]{3,2,1,0:T(8,128)} %refs_2_.1), custom_call_target="tpu_custom_call" | custom-call | tf_op jit(solution)/shard_map/merge/pallas_call | solution.py:269
  151.9 3.0 %copy.7 = f32[1,2,240,1024]{3,2,1,0:T(8,128)} copy(f32[1,2,240,1024]{3,2,1,0:T(8,128)} %get-tuple-element.8) | data formatting | bytes 3932160

commit v2 on v1

--- a/solution.py
+++ b/solution.py
@@ -9,6 +9,7 @@
 F32 = jnp.float32
 BF16 = jnp.bfloat16
 NB = 128
+R = 32
 G = 8
 Y = 4
 ZH = 4
@@ -16,36 +17,52 @@
 STEPS = ((0, 1), (0, 3), (0, 2), (1, 0), (3, 0), (1, 1), (1, 3), (3, 1), (3, 3), (1, 2), (3, 2), (2, 0), (2, 1), (2, 3), (2, 2))
 
 
-def sweep_tile(tile):
+def sweep_tile(tile, one):
     row = lax.broadcasted_iota(jnp.int32, (G, NB), 0)
     lane = lax.broadcasted_iota(jnp.int32, (G, NB), 1)
+    prow = lax.broadcasted_iota(jnp.int32, (R, NB), 0)
+    plane = lax.broadcasted_iota(jnp.int32, (R, NB), 1)
     wide = lax.broadcasted_iota(jnp.int32, (NB, NB), 1)
-    for k in range(0, NB, G):
-        cols = [jnp.broadcast_to(tile[:, k + u : k + u + 1], (NB, NB)) for u in range(G)]
-        d = {(t, u): jnp.broadcast_to(cols[u][k + t : k + t + 1, :], (G, NB)) for u in range(G) for t in range(u + 1)}
-        inside = (lane >= k) & (lane < k + G)
-        pivots = jnp.where(inside, jnp.where(lane - k == row, -1.0, 0.0), tile[k : k + G, :])
-        v = [jnp.broadcast_to(pivots[t : t + 1, :], (G, NB)) for t in range(G)]
-        r, low = [None] * G, {}
-        for t in range(G):
-            r[t] = 1.0 / d[t, t]
-            for u in range(t + 1, G):
-                low[t, u] = d[t, u] * r[t]
-            for u in range(t + 1, G):
-                for x in range(u, G):
-                    d[u, x] = d[u, x] - low[t, u] * d[t, x]
-                v[u] = v[u] - low[t, u] * v[t]
-        w = [v[t] * r[t] for t in range(G)]
-        for t in range(G - 1, 0, -1):
-            for u in range(t):
-                w[u] = w[u] - low[u, t] * w[t]
-        acc = jnp.where((wide >= k) & (wide < k + G), 0.0, tile)
-        for t in range(G):
-            acc = acc - cols[t] * jnp.broadcast_to(w[t][0:1, :], (NB, NB))
-        packed = w[0]
-        for t in range(1, G):
-            packed = jnp.where(row == t, w[t], packed)
-        tile = jnp.concatenate([x for x in (acc[:k], packed, acc[k + G :]) if x.shape[0]], axis=0)
+    for p in range(0, NB, R):
+        rows = tile[p : p + R, :]
+        before = jnp.where((plane >= p) & (plane < p + R), jnp.where(plane - p == prow, -1.0, 0.0), rows)
+        for g in range(0, R, G):
+            k = p + g
+            cols = [jnp.broadcast_to(rows[:, k + u : k + u + 1], (R, NB)) for u in range(G)]
+            pivots = rows[g : g + G, :]
+            inside = (lane >= k) & (lane < k + G)
+            marked = jnp.where(inside, jnp.where(lane - k == row, -1.0, 0.0), pivots)
+            v = [jnp.broadcast_to(marked[t : t + 1, :], (G, NB)) for t in range(G)]
+            d = {}
+            for t in range(G):
+                full = jnp.broadcast_to(pivots[t : t + 1, :], (G, NB)) * one
+                for u in range(t, G):
+                    d[t, u] = jnp.broadcast_to(full[:, k + u : k + u + 1], (G, NB))
+            r, low = [None] * G, {}
+            for t in range(G):
+                r[t] = 1.0 / d[t, t]
+                for u in range(t + 1, G):
+                    low[t, u] = d[t, u] * r[t]
+                for u in range(t + 1, G):
+                    for x in range(u, G):
+                        d[u, x] = d[u, x] - low[t, u] * d[t, x]
+                    v[u] = v[u] - low[t, u] * v[t]
+            w = [v[t] * r[t] for t in range(G)]
+            for t in range(G - 1, 0, -1):
+                for u in range(t):
+                    w[u] = w[u] - low[u, t] * w[t]
+            packed = w[0]
+            for t in range(1, G):
+                packed = jnp.where(row == t, w[t], packed)
+            acc = jnp.where((plane >= k) & (plane < k + G), 0.0, rows)
+            for t in range(G):
+                acc = acc - cols[t] * jnp.broadcast_to(w[t][0:1, :], (R, NB))
+            rows = jnp.concatenate([x for x in (acc[:g], packed, acc[g + G :]) if x.shape[0]], axis=0)
+        rest = jnp.where((wide >= p) & (wide < p + R), 0.0, tile)
+        rest = rest - lax.dot_general(
+            before, rows, (((0,), (0,)), ((), ())), precision=lax.Precision.HIGHEST, preferred_element_type=F32
+        )
+        tile = jnp.concatenate([x for x in (rest[:p], rows, rest[p + R :]) if x.shape[0]], axis=0)
     return tile
 
 
@@ -61,8 +78,8 @@
 
 
 def kernel(scale, panel_ref, in_ref, shared_ref, out_ref, mean_ref, schur, inv, rows_a, pieces, cols_b, xt_hi, xt_lo,
-           half_in, acc, sum_r, sum_p, sum_s, half_s, half_r, sz_s, sz_r, sy_s, sy_r, sx_s, sx_r, az_s, az_r, ay_s, ay_r,
-           b_s, b_r, bx_s, bx_r, pr_s, pr_r, pp_s, pp_r, ps_s, ps_r):
+           half_in, product, one, acc, sum_r, sum_p, sum_s, half_s, half_r, sz_s, sz_r, sy_s, sy_r, sx_s, sx_r, az_s, az_r, ah_s, ah_r, ay_s, ay_r,
+           b_s, b_r, bx_s, bx_r, pr_s, pr_r, pp_s, pp_r, ps_s, ps_r, o_s):
     me = lax.axis_index("rows")
     side = lax.axis_index("side")
     pair = lax.axis_index("pair")
@@ -101,7 +118,6 @@
         pl.semaphore_signal(barrier, inc=1, device_id={"rows": at(dz, dy)}, device_id_type=MESH)
     for o in range(1, pairs):
         pl.semaphore_signal(barrier, inc=1, device_id={"pair": lax.rem(pair + o, pairs)}, device_id_type=MESH)
-    pl.semaphore_wait(barrier, ROWS + pairs - 1)
 
     def strip(ref, r, s):
         return ref.at[pl.ds(pl.multiple_of((r * 2 + s) * half, 8), half), :]
@@ -109,8 +125,19 @@
     def panel_at(r):
         return rows_a.at[pl.ds(pl.multiple_of(r * 64, 64), 64), :]
 
+    def half_panel_at(r, h):
+        return rows_a.at[pl.ds(pl.multiple_of(r * 64 + h * 32, 32), 32), :]
+
     def columns_at(s, r):
         return cols_b.at[s, pl.ds(pl.multiple_of(r * 48, 16), 48), :]
+
+    for r in range(ROWS):
+        pieces[r, :, 0:width] = in_ref[0, :, r * width : (r + 1) * width]
+        pieces[r, :, width:256] = jnp.zeros((48, 256 - width), F32)
+    panel_at(me)[...] = panel_ref[0]
+    columns_at(side, me)[...] = pieces[me]
+    one[...] = jnp.ones((G, NB), F32)
+    pl.semaphore_wait(barrier, ROWS + pairs - 1)
 
     theirs = shared_ref.at[0, 0, pl.ds(pl.multiple_of((1 - side) * half, 8), half), :]
     send(theirs, half_in, half_s, half_r, sibling)
@@ -124,13 +151,8 @@
     send(mine, mine, sx_s.at[0], sx_r.at[0], sibling)
 
     panel = panel_ref.at[0]
-    for i, dz in enumerate((1, 3, 2)):
+    for i, dz in enumerate((1, 3)):
         send(panel, panel_at(me), az_s.at[i], az_r.at[i], {"rows": at(dz, 0)})
-    for r in range(ROWS):
-        pieces[r, :, 0:width] = in_ref[0, :, r * width : (r + 1) * width]
-        pieces[r, :, width:256] = jnp.zeros((48, 256 - width), F32)
-    panel_at(me)[...] = panel_ref[0]
-    columns_at(side, me)[...] = pieces[me]
 
     for i, dz in enumerate((1, 3, 2)):
         got = strip(schur, back(dz, 0), side)
@@ -138,10 +160,14 @@
         for j, dy in enumerate((1, 3, 2)):
             send(got, got, sy_s.at[i + 1, j], sy_r.at[i + 1, j], {"rows": at(0, dy)})
         send(got, got, sx_s.at[i + 1], sx_r.at[i + 1], sibling)
+
+    def columns_copy(i, dz, dy):
+        return remote(pieces.at[at(dz, dy)], columns_at(side, me), b_s.at[i], b_r.at[i], {"rows": at(dz, dy)})
+
+    for i in range(11):
+        columns_copy(i, *STEPS[i]).start()
     for j, dy in enumerate((1, 3, 2)):
         send(panel, panel_at(me), ay_s.at[0, j], ay_r.at[0, j], {"rows": at(0, dy)})
-    for i, (dz, dy) in enumerate(STEPS):
-        send(pieces.at[at(dz, dy)], columns_at(side, me), b_s.at[i], b_r.at[i], {"rows": at(dz, dy)})
     for i, dz in enumerate((0, 1, 3, 2)):
         for j, dy in enumerate((1, 3, 2)):
             got = strip(schur, back(dz, dy), side)
@@ -159,10 +185,16 @@
             remote(got, got, ay_s.at[i + 1, j], ay_r.at[i + 1, j], {"rows": at(0, dy)}) for j, dy in enumerate((1, 3, 2))
         ]
 
-    def relay_rows(i, dz):
-        arrived(panel_at(back(dz, 0)), az_s.at[i], az_r.at[i])
+    def start_rows(i, dz):
         for copy in onward_rows(i, dz):
             copy.start()
+
+    def half_copies():
+        first, last = half_panel_at(back(1, 0), 0), half_panel_at(back(3, 0), 1)
+        return [
+            remote(first, first, ah_s.at[0], ah_r.at[0], {"rows": at(1, 0)}),
+            remote(last, last, ah_s.at[1], ah_r.at[1], {"rows": at(3, 0)}),
+        ]
 
     def onward_columns(i, dz, dy):
         got = columns_at(side, back(dz, dy))
@@ -182,26 +214,29 @@
     def _(b):
         @pl.when(b == 1)
         def _():
-            relay_rows(0, 1)
-            relay_rows(1, 3)
-
-        @pl.when(b == 2)
-        def _():
-            relay_rows(2, 2)
-
-        @pl.when(b == 3)
+            for i, dz in enumerate((1, 3)):
+                arrived(panel_at(back(dz, 0)), az_s.at[i], az_r.at[i])
+            for copy in half_copies():
+                copy.start()
+            for i in range(11, 15):
+                columns_copy(i, *STEPS[i]).start()
+            start_rows(0, 1)
+            start_rows(1, 3)
+
+        @pl.when(b == 4)
         def _():
             own_columns().start()
-            for i in range(3):
+            for i in range(11):
                 relay_columns(i, *STEPS[i])
 
         @pl.when(b == 5)
         def _():
-            for i in range(3, 11):
-                relay_columns(i, *STEPS[i])
+            for h in range(2):
+                arrived(half_panel_at(back(2, 0), h), ah_s.at[h], ah_r.at[h])
+            start_rows(2, 2)
 
         block = pl.ds(pl.multiple_of(b * NB, NB), NB)
-        swept = sweep_tile(inv[block, block])
+        swept = sweep_tile(inv[block, block], one[...])
         eye = lax.broadcasted_iota(jnp.int32, (NB, NB), 0) == lax.broadcasted_iota(jnp.int32, (NB, NB), 1)
         column = inv[:, block]
         inv[block, block] = jnp.where(eye, -1.0, 0.0)
@@ -210,21 +245,26 @@
         inv[...] = inv[...] + jnp.dot(column, w, precision=lax.Precision.HIGHEST, preferred_element_type=F32)
         inv[block, :] = -w
 
+    inverse = split(inv[...])
     for i in range(11, 15):
         relay_columns(i, *STEPS[i])
+
+    def solve(b):
+        xt_hi[b], xt_lo[b] = split(dot3(split(cols_b[b].T), inverse, ((1,), (0,))))
+
+    solve(side)
     arrived(columns_at(1 - side, me), bx_s.at[15], bx_r.at[15])
     for i, (dz, dy) in enumerate(STEPS):
         arrived(columns_at(1 - side, back(dz, dy)), bx_s.at[i], bx_r.at[i])
+    solve(1 - side)
     for i, dz in enumerate((0, 1, 3, 2)):
         for j, dy in enumerate((1, 3, 2)):
             arrived(panel_at(back(dz, dy)), ay_s.at[i, j], ay_r.at[i, j])
 
-    inverse = split(inv[...])
-    for b in range(2):
-        x = dot3(split(cols_b[b].T), inverse, ((1,), (0,)))
-        xt_hi[b], xt_lo[b] = split(x)
-
     acc[...] = jnp.zeros((8, 128), F32)
+
+    def out_copy(i, tile):
+        return pltpu.make_async_copy(product.at[:, :, tile], out_ref.at[0, :, :, tile], o_s.at[i])
 
     @pl.loop(0, 4)
     def _(i):
@@ -232,9 +272,10 @@
         a = split(rows_a[tile, :])
         for b in range(2):
             c = dot3((xt_hi[b], xt_lo[b]), a, ((1,), (1,)))[:width]
-            out_ref[0, b, :, tile] = c
+            product[b, :, tile] = c
             s = jnp.sum((c * c).reshape(width // 8, 8, 256), axis=0)
             acc[...] = acc[...] + (s[:, :128] + s[:, 128:])
+        out_copy(i, tile).start()
 
     sum_r[me] = acc[...]
     for i, (dz, dy) in enumerate(STEPS):
@@ -251,28 +292,33 @@
     send(sum_s.at[side], sum_s.at[side], ps_s, ps_r, sibling)
     arrived(sum_s.at[1 - side], ps_s, ps_r)
     mean_ref[0, 0] = jnp.sum(sum_s[0] + sum_s[1]) * scale
+    sends.extend(half_copies())
     for i, dz in enumerate((1, 3, 2)):
         sends.extend(onward_rows(i, dz))
     for i, (dz, dy) in enumerate(STEPS):
-        sends.append(onward_columns(i, dz, dy))
+        sends.extend([columns_copy(i, dz, dy), onward_columns(i, dz, dy)])
     sends.append(own_columns())
     for copy in sends:
         copy.wait_send()
+    for i in range(4):
+        out_copy(i, pl.ds(i * 256, 256)).wait()
 
 
 def body(face_out, face_in, face_shared):
     dma = pltpu.SemaphoreType.DMA
     vmem = pltpu.VMEM
-    sems = [dma, dma, dma((3,)), dma((3,)), dma((4, 3)), dma((4, 3)), dma((16,)), dma((16,)), dma((3,)), dma((3,)), dma((4, 3)),
-            dma((4, 3)), dma((15,)), dma((15,)), dma((16,)), dma((16,)), dma((15,)), dma((15,)), dma((16,)), dma((16,)), dma, dma]
+    sems = [dma, dma, dma((3,)), dma((3,)), dma((4, 3)), dma((4, 3)), dma((16,)), dma((16,)), dma((2,)), dma((2,)), dma((2,)),
+            dma((2,)), dma((4, 3)), dma((4, 3)), dma((15,)), dma((15,)), dma((16,)), dma((16,)), dma((15,)), dma((15,)),
+            dma((16,)), dma((16,)), dma, dma, dma((4,))]
     entries = 16 * 2 * 3840 * 2048
     out, mean = pl.pallas_call(
         lambda *refs: kernel(1.0 / entries, *refs),
         out_shape=(jax.ShapeDtypeStruct((1, 2, 240, 1024), F32), jax.ShapeDtypeStruct((1, 1), F32)),
         in_specs=[pl.BlockSpec(memory_space=vmem)] * 3,
-        out_specs=(pl.BlockSpec(memory_space=vmem), pl.BlockSpec(memory_space=pltpu.SMEM)),
+        out_specs=(pl.BlockSpec(memory_space=pl.ANY), pl.BlockSpec(memory_space=pltpu.SMEM)),
         scratch_shapes=[vmem((768, 768), F32), vmem((768, 768), F32), vmem((1024, 768), F32), vmem((16, 48, 256), F32),
                         vmem((2, 768, 256), F32), vmem((2, 256, 768), BF16), vmem((2, 256, 768), BF16), vmem((24, 768), F32),
+                        vmem((2, 240, 1024), F32), vmem((G, NB), F32),
                         vmem((8, 128), F32), vmem((16, 8, 128), F32), vmem((16, 8, 128), F32), vmem((2, 8, 128), F32)] + sems,
         compiler_params=pltpu.CompilerParams(collective_id=0, has_side_effects=True, vmem_limit_bytes=56 << 20),
         name="merge",

time: 157 us -> 132 us (0.84)
  Pallas kernels: 151 us -> 127 us
    pallas_call x1, Pallas kernels: 151 us -> 127 us  [body(): pl.pallas_call(lambda *refs: kernel(1.0 / entries, *refs), out_shape=(jax...]
where the time goes in v2:
time: 132 us
  Pallas kernels  127 us (96%)
  local copies, waits for them, and re-layouts  3.04 us (2%)
  between operations  2.39 us (2%)
    pallas_call x1, Pallas kernels, body(): pl.pallas_call(lambda *refs: kernel(1.0 / entries, *refs), out_shape=(jax...  127 us
    unnamed x1, local copies, waits for them, and re-layouts  3.04 us

profile of v2, /device:TPU:1, one launch (start us, length us, event | category | flops | bytes accessed | tf_op | source)
XLA Modules:
  0.0 132.3 jit_solution(9388188466989479027)
XLA Ops:
  0.6 126.8 %merge.1 = (f32[1,2,240,1024]{3,2,1,0:T(8,128)}, f32[1,1]{1,0:T(1,128)}) custom-call(f32[1,64,768]{2,1,0:T(8,128)} %refs_0_.1, f32[1,48,3840]{2,1,0:T(8,128)} %refs_1_.1, f32[1,1,48,768]{3,2,1,0:T(8,128)} %refs_2_.1), custom_call_target="tpu_custom_call" | custom-call | tf_op jit(solution)/shard_map/merge/pallas_call | solution.py:314
  127.5 3.0 %copy.7 = f32[1,2,240,1024]{3,2,1,0:T(8,128)} copy(f32[1,2,240,1024]{3,2,1,0:T(8,128)} %get-tuple-element.8) | data formatting | bytes 3932160

commit v3 on v2

--- a/solution.py
+++ b/solution.py
@@ -13,6 +13,7 @@
 G = 8
 Y = 4
 ZH = 4
+Z = 16
 ROWS = Y * ZH
 STEPS = ((0, 1), (0, 3), (0, 2), (1, 0), (3, 0), (1, 1), (1, 3), (3, 1), (3, 3), (1, 2), (3, 2), (2, 0), (2, 1), (2, 3), (2, 2))
 
@@ -78,8 +79,8 @@
 
 
 def kernel(scale, panel_ref, in_ref, shared_ref, out_ref, mean_ref, schur, inv, rows_a, pieces, cols_b, xt_hi, xt_lo,
-           half_in, product, one, acc, sum_r, sum_p, sum_s, half_s, half_r, sz_s, sz_r, sy_s, sy_r, sx_s, sx_r, az_s, az_r, ah_s, ah_r, ay_s, ay_r,
-           b_s, b_r, bx_s, bx_r, pr_s, pr_r, pp_s, pp_r, ps_s, ps_r, o_s):
+           half_in, one, acc, sum_z, sum_xy, half_s, half_r, sz_s, sz_r, sy_s, sy_r, sx_s, sx_r, az_s, az_r, ah_s, ah_r, ay_s, ay_r,
+           b_s, b_r, bx_s, bx_r, ay4_s, ay4_r, pz_s, pz_r, pxy_s, pxy_r):
     me = lax.axis_index("rows")
     side = lax.axis_index("side")
     pair = lax.axis_index("pair")
@@ -87,13 +88,21 @@
     n = 768
     half = 24
     width = 240
-    pairs = 16
+    z, x = zh * Y + lax.rem(pair, Y), pair // Y
 
     def at(dz, dy):
         return lax.rem(zh + dz, ZH) * Y + lax.rem(y + dy, Y)
 
     def back(dz, dy):
         return lax.rem(zh + ZH - dz, ZH) * Y + lax.rem(y + Y - dy, Y)
+
+    def on_line(o):
+        there = lax.rem(z + o, Z)
+        return {"rows": there // ZH * Y + y, "pair": x * Y + lax.rem(there, ZH)}
+
+    def on_plane(dx, dy, other):
+        there = {"rows": at(0, dy), "pair": lax.rem(x + dx, Y) * Y + lax.rem(pair, Y)}
+        return there | ({"side": 1 - side} if other else {})
 
     sibling = {"side": 1 - side}
 
@@ -116,8 +125,10 @@
     pl.semaphore_signal(barrier, inc=1, device_id=sibling, device_id_type=MESH)
     for dz, dy in STEPS:
         pl.semaphore_signal(barrier, inc=1, device_id={"rows": at(dz, dy)}, device_id_type=MESH)
-    for o in range(1, pairs):
-        pl.semaphore_signal(barrier, inc=1, device_id={"pair": lax.rem(pair + o, pairs)}, device_id_type=MESH)
+    line = [on_line(o) for o in range(1, Z) if o % ZH]
+    plane = [on_plane(dx, dy, False) for dx, dy in STEPS if dx] + [on_plane(dx, dy, True) for dx, dy in STEPS]
+    for device in line + plane:
+        pl.semaphore_signal(barrier, inc=1, device_id=device, device_id_type=MESH)
 
     def strip(ref, r, s):
         return ref.at[pl.ds(pl.multiple_of((r * 2 + s) * half, 8), half), :]
@@ -125,8 +136,8 @@
     def panel_at(r):
         return rows_a.at[pl.ds(pl.multiple_of(r * 64, 64), 64), :]
 
-    def half_panel_at(r, h):
-        return rows_a.at[pl.ds(pl.multiple_of(r * 64 + h * 32, 32), 32), :]
+    def quarter_at(r, q):
+        return rows_a.at[pl.ds(pl.multiple_of(r * 64 + q * 16, 16), 16), :]
 
     def columns_at(s, r):
         return cols_b.at[s, pl.ds(pl.multiple_of(r * 48, 16), 48), :]
@@ -137,7 +148,13 @@
     panel_at(me)[...] = panel_ref[0]
     columns_at(side, me)[...] = pieces[me]
     one[...] = jnp.ones((G, NB), F32)
-    pl.semaphore_wait(barrier, ROWS + pairs - 1)
+    pl.semaphore_wait(barrier, ROWS + len(line) + len(plane))
+
+    def columns_copy(i, dz, dy):
+        return remote(pieces.at[at(dz, dy)], columns_at(side, me), b_s.at[i], b_r.at[i], {"rows": at(dz, dy)})
+
+    for i in (3, 4):
+        columns_copy(i, *STEPS[i]).start()
 
     theirs = shared_ref.at[0, 0, pl.ds(pl.multiple_of((1 - side) * half, 8), half), :]
     send(theirs, half_in, half_s, half_r, sibling)
@@ -161,10 +178,7 @@
             send(got, got, sy_s.at[i + 1, j], sy_r.at[i + 1, j], {"rows": at(0, dy)})
         send(got, got, sx_s.at[i + 1], sx_r.at[i + 1], sibling)
 
-    def columns_copy(i, dz, dy):
-        return remote(pieces.at[at(dz, dy)], columns_at(side, me), b_s.at[i], b_r.at[i], {"rows": at(dz, dy)})
-
-    for i in range(11):
+    for i in (0, 1, 2, *range(5, 15)):
         columns_copy(i, *STEPS[i]).start()
     for j, dy in enumerate((1, 3, 2)):
         send(panel, panel_at(me), ay_s.at[0, j], ay_r.at[0, j], {"rows": at(0, dy)})
@@ -190,11 +204,21 @@
             copy.start()
 
     def half_copies():
-        first, last = half_panel_at(back(1, 0), 0), half_panel_at(back(3, 0), 1)
         return [
-            remote(first, first, ah_s.at[0], ah_r.at[0], {"rows": at(1, 0)}),
-            remote(last, last, ah_s.at[1], ah_r.at[1], {"rows": at(3, 0)}),
+            remote(
+                quarter_at(back(dz, 0), q), quarter_at(back(dz, 0), q), ah_s.at[q], ah_r.at[q], {"rows": at(dz, 0)}
+            )
+            for dz, q in ((1, 0), (3, 3), (1, 1), (3, 2))
         ]
+
+    def onward_quarter(q):
+        got = quarter_at(back(2, 0), q)
+        return [remote(got, got, ay4_s.at[q, j], ay4_r.at[q, j], {"rows": at(0, dy)}) for j, dy in enumerate((1, 3, 2))]
+
+    def relay_quarter(q):
+        arrived(quarter_at(back(2, 0), q), ah_s.at[q], ah_r.at[q])
+        for copy in onward_quarter(q):
+            copy.start()
 
     def onward_columns(i, dz, dy):
         got = columns_at(side, back(dz, dy))
@@ -218,22 +242,14 @@
                 arrived(panel_at(back(dz, 0)), az_s.at[i], az_r.at[i])
             for copy in half_copies():
                 copy.start()
-            for i in range(11, 15):
-                columns_copy(i, *STEPS[i]).start()
             start_rows(0, 1)
             start_rows(1, 3)
 
-        @pl.when(b == 4)
+        @pl.when(b == 5)
         def _():
             own_columns().start()
             for i in range(11):
                 relay_columns(i, *STEPS[i])
-
-        @pl.when(b == 5)
-        def _():
-            for h in range(2):
-                arrived(half_panel_at(back(2, 0), h), ah_s.at[h], ah_r.at[h])
-            start_rows(2, 2)
 
         block = pl.ds(pl.multiple_of(b * NB, NB), NB)
         swept = sweep_tile(inv[block, block], one[...])
@@ -253,73 +269,84 @@
         xt_hi[b], xt_lo[b] = split(dot3(split(cols_b[b].T), inverse, ((1,), (0,))))
 
     solve(side)
+    for q in (0, 3):
+        relay_quarter(q)
     arrived(columns_at(1 - side, me), bx_s.at[15], bx_r.at[15])
     for i, (dz, dy) in enumerate(STEPS):
         arrived(columns_at(1 - side, back(dz, dy)), bx_s.at[i], bx_r.at[i])
     solve(1 - side)
-    for i, dz in enumerate((0, 1, 3, 2)):
+    for q in (1, 2):
+        relay_quarter(q)
+    for i, dz in enumerate((0, 1, 3)):
         for j, dy in enumerate((1, 3, 2)):
             arrived(panel_at(back(dz, dy)), ay_s.at[i, j], ay_r.at[i, j])
 
     acc[...] = jnp.zeros((8, 128), F32)
 
-    def out_copy(i, tile):
-        return pltpu.make_async_copy(product.at[:, :, tile], out_ref.at[0, :, :, tile], o_s.at[i])
-
-    @pl.loop(0, 4)
+    def tile_of(i):
+        return pl.ds(pl.multiple_of(lax.rem(zh + i + i // 2 - i // 3 * 2, ZH) * 256, 256), 256)
+
+    def out_copy(i):
+        return pltpu.make_async_copy(product.at[:, :, tile_of(i)], out_ref.at[0, :, :, tile_of(i)], o_s.at[i])
+
+    @pl.loop(0, ZH)
     def _(i):
-        tile = pl.ds(pl.multiple_of(i * 256, 256), 256)
+        @pl.when(i == ZH - 1)
+        def _():
+            for q in (0, 3, 1, 2):
+                for j, dy in enumerate((1, 3, 2)):
+                    arrived(quarter_at(back(2, dy), q), ay4_s.at[q, j], ay4_r.at[q, j])
+
+        tile = tile_of(i)
         a = split(rows_a[tile, :])
         for b in range(2):
             c = dot3((xt_hi[b], xt_lo[b]), a, ((1,), (1,)))[:width]
-            product[b, :, tile] = c
+            out_ref[0, b, :, tile] = c
             s = jnp.sum((c * c).reshape(width // 8, 8, 256), axis=0)
             acc[...] = acc[...] + (s[:, :128] + s[:, 128:])
-        out_copy(i, tile).start()
-
-    sum_r[me] = acc[...]
-    for i, (dz, dy) in enumerate(STEPS):
-        send(acc, sum_r.at[me], pr_s.at[i], pr_r.at[i], {"rows": at(dz, dy)})
-    for i, (dz, dy) in enumerate(STEPS):
-        arrived(sum_r.at[back(dz, dy)], pr_s.at[i], pr_r.at[i])
-    sum_p[pair] = jnp.sum(sum_r[...], axis=0)
-    for o in range(1, pairs):
-        send(sum_p.at[pair], sum_p.at[pair], pp_s.at[o], pp_r.at[o], {"pair": lax.rem(pair + o, pairs)})
-    for o in range(1, pairs):
-        arrived(sum_p.at[lax.rem(pair + pairs - o, pairs)], pp_s.at[o], pp_r.at[o])
-    total = jnp.sum(sum_p[...], axis=0)
-    sum_s[side] = total
-    send(sum_s.at[side], sum_s.at[side], ps_s, ps_r, sibling)
-    arrived(sum_s.at[1 - side], ps_s, ps_r)
-    mean_ref[0, 0] = jnp.sum(sum_s[0] + sum_s[1]) * scale
+
+    sum_z[z] = acc[...]
+    for o in range(1, Z):
+        send(acc, sum_z.at[z], pz_s.at[o], pz_r.at[o], on_line(o))
+    for o in range(1, Z):
+        arrived(sum_z.at[lax.rem(z + Z - o, Z)], pz_s.at[o], pz_r.at[o])
+    mine = sum_xy.at[side, x * Y + y]
+    mine[...] = jnp.sum(sum_z[...], axis=0)
+    for other in range(2):
+        for i, (dx, dy) in enumerate(((0, 0), *STEPS)[1 - other :]):
+            send(mine, mine, pxy_s.at[other, i], pxy_r.at[other, i], on_plane(dx, dy, other))
+    for other in range(2):
+        for i, (dx, dy) in enumerate(((0, 0), *STEPS)[1 - other :]):
+            slot = lax.rem(x + Y - dx, Y) * Y + lax.rem(y + Y - dy, Y)
+            arrived(sum_xy.at[1 - side if other else side, slot], pxy_s.at[other, i], pxy_r.at[other, i])
+    mean_ref[0, 0] = jnp.sum(jnp.sum(sum_xy[...], axis=(0, 1))) * scale
     sends.extend(half_copies())
-    for i, dz in enumerate((1, 3, 2)):
+    for i, dz in enumerate((1, 3)):
         sends.extend(onward_rows(i, dz))
+    for q in range(4):
+        sends.extend(onward_quarter(q))
     for i, (dz, dy) in enumerate(STEPS):
         sends.extend([columns_copy(i, dz, dy), onward_columns(i, dz, dy)])
     sends.append(own_columns())
     for copy in sends:
         copy.wait_send()
-    for i in range(4):
-        out_copy(i, pl.ds(i * 256, 256)).wait()
 
 
 def body(face_out, face_in, face_shared):
     dma = pltpu.SemaphoreType.DMA
     vmem = pltpu.VMEM
-    sems = [dma, dma, dma((3,)), dma((3,)), dma((4, 3)), dma((4, 3)), dma((16,)), dma((16,)), dma((2,)), dma((2,)), dma((2,)),
-            dma((2,)), dma((4, 3)), dma((4, 3)), dma((15,)), dma((15,)), dma((16,)), dma((16,)), dma((15,)), dma((15,)),
-            dma((16,)), dma((16,)), dma, dma, dma((4,))]
+    shapes = ((), (3,), (4, 3), (16,), (2,), (4,), (3, 3), (15,), (16,), (4, 3), (Z,), (2, 16))
+    sems = [dma(s) if s else dma for s in shapes for _ in range(2)]
     entries = 16 * 2 * 3840 * 2048
     out, mean = pl.pallas_call(
         lambda *refs: kernel(1.0 / entries, *refs),
-        out_shape=(jax.ShapeDtypeStruct((1, 2, 240, 1024), F32), jax.ShapeDtypeStruct((1, 1), F32)),
+        out_shape=(vmem((1, 2, 240, 1024), F32), jax.ShapeDtypeStruct((1, 1), F32)),
         in_specs=[pl.BlockSpec(memory_space=vmem)] * 3,
-        out_specs=(pl.BlockSpec(memory_space=pl.ANY), pl.BlockSpec(memory_space=pltpu.SMEM)),
+        out_specs=(pl.BlockSpec(memory_space=vmem), pl.BlockSpec(memory_space=pltpu.SMEM)),
         scratch_shapes=[vmem((768, 768), F32), vmem((768, 768), F32), vmem((1024, 768), F32), vmem((16, 48, 256), F32),
                         vmem((2, 768, 256), F32), vmem((2, 256, 768), BF16), vmem((2, 256, 768), BF16), vmem((24, 768), F32),
-                        vmem((2, 240, 1024), F32), vmem((G, NB), F32),
-                        vmem((8, 128), F32), vmem((16, 8, 128), F32), vmem((16, 8, 128), F32), vmem((2, 8, 128), F32)] + sems,
+                        vmem((G, NB), F32),
+                        vmem((8, 128), F32), vmem((Z, 8, 128), F32), vmem((2, 16, 8, 128), F32)] + sems,
         compiler_params=pltpu.CompilerParams(collective_id=0, has_side_effects=True, vmem_limit_bytes=56 << 20),
         name="merge",
     )(face_out, face_in, face_shared)

time: 132 us -> 141 us (1.068)
  Pallas kernels: 127 us -> 138 us
  local copies, waits for them, and re-layouts: 3.04 us -> 1.27 us
    pallas_call x1, Pallas kernels: 127 us -> 138 us  [body(): pl.pallas_call(lambda *refs: kernel(1.0 / entries, *refs), out_shape=(vme...]
    unnamed x1, local copies, waits for them, and re-layouts: 3.04 us -> 1.27 us
where the time goes in v3:
time: 141 us
  Pallas kernels  138 us (98%)
  between operations  2.33 us (2%)
    pallas_call x1, Pallas kernels, body(): pl.pallas_call(lambda *refs: kernel(1.0 / entries, *refs), out_shape=(vme...  138 us

profile of v3, /device:TPU:1, one launch (start us, length us, event | category | flops | bytes accessed | tf_op | source)
XLA Modules:
  0.0 141.3 jit_solution(13517721972815202393)
XLA Ops:
  0.6 137.7 %merge.1 = (f32[1,2,240,1024]{3,2,1,0:T(8,128)S(1)}, f32[1,1]{1,0:T(1,128)}) custom-call(f32[1,64,768]{2,1,0:T(8,128)} %refs_0_.1, f32[1,48,3840]{2,1,0:T(8,128)} %refs_1_.1, f32[1,1,48,768]{3,2,1,0:T(8,128)} %refs_2_.1), custom_call_target="tpu_custom_call" | custom-call | tf_op jit(solution)/shard_map/merge/pallas_call | solution.py:341
  138.3 1.3 copy.7

commit v4 on v2

--- a/solution.py
+++ b/solution.py
@@ -78,8 +78,8 @@
 
 
 def kernel(scale, panel_ref, in_ref, shared_ref, out_ref, mean_ref, schur, inv, rows_a, pieces, cols_b, xt_hi, xt_lo,
-           half_in, product, one, acc, sum_r, sum_p, sum_s, half_s, half_r, sz_s, sz_r, sy_s, sy_r, sx_s, sx_r, az_s, az_r, ah_s, ah_r, ay_s, ay_r,
-           b_s, b_r, bx_s, bx_r, pr_s, pr_r, pp_s, pp_r, ps_s, ps_r, o_s):
+           half_in, one, acc, sum_r, sum_p, sum_s, half_s, half_r, sz_s, sz_r, sy_s, sy_r, sx_s, sx_r, az_s, az_r, ah_s, ah_r, ay_s, ay_r,
+           b_s, b_r, bx_s, bx_r, pr_s, pr_r, pp_s, pp_r, ps_s, ps_r):
     me = lax.axis_index("rows")
     side = lax.axis_index("side")
     pair = lax.axis_index("pair")
@@ -272,10 +272,9 @@
         a = split(rows_a[tile, :])
         for b in range(2):
             c = dot3((xt_hi[b], xt_lo[b]), a, ((1,), (1,)))[:width]
-            product[b, :, tile] = c
+            out_ref[0, b, :, tile] = c
             s = jnp.sum((c * c).reshape(width // 8, 8, 256), axis=0)
             acc[...] = acc[...] + (s[:, :128] + s[:, 128:])
-        out_copy(i, tile).start()
 
     sum_r[me] = acc[...]
     for i, (dz, dy) in enumerate(STEPS):
@@ -300,8 +299,6 @@
     sends.append(own_columns())
     for copy in sends:
         copy.wait_send()
-    for i in range(4):
-        out_copy(i, pl.ds(i * 256, 256)).wait()
 
 
 def body(face_out, face_in, face_shared):
@@ -309,16 +306,16 @@
     vmem = pltpu.VMEM
     sems = [dma, dma, dma((3,)), dma((3,)), dma((4, 3)), dma((4, 3)), dma((16,)), dma((16,)), dma((2,)), dma((2,)), dma((2,)),
             dma((2,)), dma((4, 3)), dma((4, 3)), dma((15,)), dma((15,)), dma((16,)), dma((16,)), dma((15,)), dma((15,)),
-            dma((16,)), dma((16,)), dma, dma, dma((4,))]
+            dma((16,)), dma((16,)), dma, dma]
     entries = 16 * 2 * 3840 * 2048
     out, mean = pl.pallas_call(
         lambda *refs: kernel(1.0 / entries, *refs),
-        out_shape=(jax.ShapeDtypeStruct((1, 2, 240, 1024), F32), jax.ShapeDtypeStruct((1, 1), F32)),
+        out_shape=(vmem((1, 2, 240, 1024), F32), jax.ShapeDtypeStruct((1, 1), F32)),
         in_specs=[pl.BlockSpec(memory_space=vmem)] * 3,
-        out_specs=(pl.BlockSpec(memory_space=pl.ANY), pl.BlockSpec(memory_space=pltpu.SMEM)),
+        out_specs=(pl.BlockSpec(memory_space=vmem), pl.BlockSpec(memory_space=pltpu.SMEM)),
         scratch_shapes=[vmem((768, 768), F32), vmem((768, 768), F32), vmem((1024, 768), F32), vmem((16, 48, 256), F32),
                         vmem((2, 768, 256), F32), vmem((2, 256, 768), BF16), vmem((2, 256, 768), BF16), vmem((24, 768), F32),
-                        vmem((2, 240, 1024), F32), vmem((G, NB), F32),
+                        vmem((G, NB), F32),
                         vmem((8, 128), F32), vmem((16, 8, 128), F32), vmem((16, 8, 128), F32), vmem((2, 8, 128), F32)] + sems,
         compiler_params=pltpu.CompilerParams(collective_id=0, has_side_effects=True, vmem_limit_bytes=56 << 20),
         name="merge",

time: 132 us -> 131 us (level)
  local copies, waits for them, and re-layouts: 3.04 us -> 1.27 us
    unnamed x1, local copies, waits for them, and re-layouts: 3.04 us -> 1.27 us
where the time goes in v4:
time: 131 us; the launch traced here: 130 us
  Pallas kernels  127 us (97%)
  between operations  2.33 us (2%)
    pallas_call x1, Pallas kernels, body(): pl.pallas_call(lambda *refs: kernel(1.0 / entries, *refs), out_shape=(vme...  127 us

profile of v4, /device:TPU:1, one launch (start us, length us, event | category | flops | bytes accessed | tf_op | source)
XLA Modules:
  0.0 130.4 jit_solution(10761771876644423978)
XLA Ops:
  0.6 126.8 %merge.1 = (f32[1,2,240,1024]{3,2,1,0:T(8,128)S(1)}, f32[1,1]{1,0:T(1,128)}) custom-call(f32[1,64,768]{2,1,0:T(8,128)} %refs_0_.1, f32[1,48,3840]{2,1,0:T(8,128)} %refs_1_.1, f32[1,1,48,768]{3,2,1,0:T(8,128)} %refs_2_.1), custom_call_target="tpu_custom_call" | custom-call | tf_op jit(solution)/shard_map/merge/pallas_call | solution.py:311
  127.4 1.3 copy.7
